TPU v7x, 256 devices: a whole 4x4x8 slice. The times are simulated.
256 devices in a mesh: leaf: 4 (over y), row: 16 (over z, core), col: 4 (over x).
Axes of the slice: x: 4, y: 4, z: 8, core: 2. Of those that a mesh axis runs over, the one named last changes fastest.
Arguments:
- anc_inverse: float32 [24, 24, 512, 512], P('leaf', None, 'row', 'col'), may hold values from -6 to 6, as said below
- struct_one: int32 [12, 5], P('leaf'), may hold values from 0 to 23, as said below
- lower_one: float32 [12, 5, 512, 512], P('leaf', None, 'row', 'col'), may hold values from -0.125 to 0.125
- pivot_inv_one: float32 [12, 512, 512], P('leaf', 'row', 'col'), may hold values from -6 to 6, as said below
- lower_two: float32 [24, 6, 512, 512], P('leaf', None, 'row', 'col'), may hold values from -0.109375 to 0.109375
- pivot_inv_two: float32 [24, 512, 512], P('leaf', 'row', 'col'), may hold values from -6 to 6, as said below
Outputs:
- offdiag_one: float32 [12, 5, 512, 512], P('leaf', None, 'row', 'col')
- diag_one: float32 [12, 512, 512], P('leaf', 'row', 'col')
- offdiag_two: float32 [24, 6, 512, 512], P('leaf', None, 'row', 'col')
- diag_two: float32 [24, 512, 512], P('leaf', 'row', 'col')
Inputs may be any that keep to these rules, and one draw needn't show every extreme that they name: `struct_one`: each row lists 5 different separator block numbers in increasing order. symmetric: anc_inverse[b, a] is the transpose of anc_inverse[a, b]. `pivot_inv_one`: every block equals its transpose. `pivot_inv_two`: every block equals its transpose.
All inputs are finite; a program needn't handle non-finite values.
Results may differ from a plain program's by a relative error of at most 0.0001.
Values sent between devices are 32-bit elements; how exact they have to be, the bound alone decides.
A program may use at most 64 MiB of HBM per device.

v0:
```python
import jax
import jax.numpy as jnp
from jax import lax
from jax.sharding import PartitionSpec as P

highest = lax.Precision.HIGHEST


def on_device(anc_inverse, struct_one, lower_one, pivot_inv_one, lower_two, pivot_inv_two):
    level_nodes, struct_len = struct_one.shape
    tile_rows = lower_one.shape[2]
    tile_cols = lower_one.shape[3]
    children = lower_two.shape[0] // level_nodes
    one_rows = lax.all_gather(lower_one, "row", axis=2, tiled=True)
    one_cols, two_cols = (
        lax.all_gather(lower_one, "col", axis=3, tiled=True),
        lax.all_gather(lower_two, "col", axis=3, tiled=True),
    )
    ancestors = lax.all_gather(anc_inverse, "leaf", axis=0, tiled=True)
    selected = ancestors[struct_one[:, :, None], struct_one[:, None, :]]
    stripes = lax.all_gather(selected, "col", axis=4, tiled=True)
    offdiag_one = -jnp.einsum("mstik,mtkj->msij", stripes, one_rows, precision=highest)
    cols_piece = one_cols
    summed_one = lax.psum_scatter(
        jnp.einsum("mski,mskj->imj", cols_piece, offdiag_one, precision=highest),
        "row",
        scatter_dimension=0,
        tiled=True,
    )
    diag_one = pivot_inv_one - jnp.transpose(summed_one, (1, 0, 2))
    parent_col = jnp.concatenate([offdiag_one, diag_one[:, None]], axis=1)
    parent_stripe = lax.all_gather(parent_col, "col", axis=3, tiled=True)
    two_rows = lax.all_gather(lower_two, "row", axis=2, tiled=True)
    rows_split = two_rows.reshape(
        level_nodes, children, struct_len + 1, two_rows.shape[2], tile_cols
    )
    cols_split = two_cols.reshape(
        level_nodes, children, struct_len + 1, tile_rows, two_cols.shape[3]
    )
    local_split = lower_two.reshape(level_nodes, children, struct_len + 1, tile_rows, tile_cols)
    upper_part = jnp.einsum(
        "mstik,mctkj->mcsij", stripes, rows_split[:, :, :struct_len], precision=highest
    )
    upper_part = upper_part + jnp.einsum(
        "msik,mckj->mcsij",
        parent_stripe[:, :struct_len],
        rows_split[:, :, struct_len],
        precision=highest,
    )
    stripe_piece = parent_stripe[:, :struct_len]
    summed_parent = lax.psum_scatter(
        jnp.einsum(
            "mqki,mcqkj->imcj", stripe_piece, local_split[:, :, :struct_len], precision=highest
        ),
        "row",
        scatter_dimension=0,
        tiled=True,
    )
    parent_row = jnp.transpose(summed_parent, (1, 2, 0, 3))
    parent_row = parent_row + jnp.einsum(
        "mik,mckj->mcij",
        parent_stripe[:, struct_len],
        rows_split[:, :, struct_len],
        precision=highest,
    )
    offdiag_split = -jnp.concatenate([upper_part, parent_row[:, :, None]], axis=2)
    cols_piece = cols_split
    summed_two = lax.psum_scatter(
        jnp.einsum("mcpki,mcpkj->imcj", cols_piece, offdiag_split, precision=highest),
        "row",
        scatter_dimension=0,
        tiled=True,
    )
    diag_two = pivot_inv_two - jnp.transpose(summed_two, (1, 2, 0, 3)).reshape(
        level_nodes * children, tile_rows, tile_cols
    )
    offdiag_two = offdiag_split.reshape(
        level_nodes * children, struct_len + 1, tile_rows, tile_cols
    )
    return (offdiag_one, diag_one, offdiag_two, diag_two)


def solution(mesh):
    placed = (
        P("leaf", None, "row", "col"),
        P("leaf", None),
        P("leaf", None, "row", "col"),
        P("leaf", "row", "col"),
        P("leaf", None, "row", "col"),
        P("leaf", "row", "col"),
    )
    return jax.shard_map(
        on_device,
        mesh=mesh,
        in_specs=placed,
        out_specs=(
            P("leaf", None, "row", "col"),
            P("leaf", "row", "col"),
            P("leaf", None, "row", "col"),
            P("leaf", "row", "col"),
        ),
        check_vma=False,
    )
```

profile of v0, /device:TPU:1, one launch (start us, length us, event | category | flops | bytes accessed | tf_op | source)
XLA Modules:
  0.0 604.5 jit_solution(8348671050504362168)
XLA Ops:
  7.2 0.7 all-gather.7.cloned.1.call-update
  8.0 0.7 all-gather.11.cloned.1.call-update
  8.7 0.1 broadcast_or_fusion
  8.8 0.1 reshape.41
  8.9 99.3 %all-gather.7.cloned.1.call-done = f32[24,24,32,128]{3,2,1,0:T(8,128)} async-done(((f32[6,24,32,128]{3,2,1,0:T(8,128)}), f32[24,24,32,128]{3,2,1,0:T(8,128)}) %all-gather.7.cloned.1.call-update) | async-done | bytes 9437200 | tf_op jit(solution)/shard_map/all_gather | solution.py:19
  108.2 5.9 gather_fusion
  114.2 13.2 %all_gather.24 = f32[3,5,32,512]{3,2,1,0:T(8,128)S(1)} all-gather(f32[3,5,32,128]{3,2,1,0:T(8,128)S(1)} %copy-done.3), channel_id=1, replica_groups=mesh['leaf'=4,'row'=16,'col'=4] {'col'}, dimensions={3}, use_global_device_ids=true | all-gather | bytes 1228800 | tf_op jit(solution)/shard_map/all_gather | solution.py:16
  127.4 26.1 %all-gather.11.cloned.1.call-done = f32[3,5,512,128]{3,2,1,0:T(8,128)} async-done(((f32[3,5,32,128]{3,2,1,0:T(8,128)}), f32[3,5,512,128]{3,2,1,0:T(8,128)}) %all-gather.11.cloned.1.call-update) | async-done | bytes 3932176 | tf_op jit(solution)/shard_map/all_gather | solution.py:14
  153.5 59.6 %all-gather.9.cloned.1.call-done = f32[3,5,5,32,512]{4,3,2,1,0:T(8,128)} async-done(((f32[3,5,5,32,128]{4,3,2,1,0:T(8,128)}), f32[3,5,5,32,512]{4,3,2,1,0:T(8,128)}) %all-gather.9.cloned.1.call-update) | async-done | bytes 4915216 | tf_op jit(solution)/shard_map/all_gather | solution.py:21
  213.1 8.0 %fusion.22 = f32[3,5,32,128]{3,2,1,0:T(8,128)S(1)} fusion(f32[3,5,5,32,512]{4,3,2,1,0:T(8,128)} %all-gather.9.cloned.1.call-done, f32[3,5,512,128]{3,2,1,0:T(8,128)} %all-gather.11.cloned.1.call-done), kind=kOutput, calls=%fused_computation.19 | convolution fusion | flops 1887498240 | bytes 9093120 | tf_op jit(solution)/shard_map/mstik,mtkj->msij/dot_general | solution.py:22
  221.1 3.6 convolution_bitcast_fusion.2
  224.8 55.9 %reduce-scatter.3.cloned.1.call-done = f32[32,3,128]{2,0,1:T(8,128)} async-done(((f32[512,3,128]{2,0,1:T(8,128)}), f32[32,3,128]{2,0,1:T(8,128)}) %reduce-scatter.3.cloned.1.call-update) | async-done | bytes 49168 | tf_op jit(solution)/shard_map/reduce_scatter | solution.py:24
  280.7 0.8 bitcast_subtract_fusion.1
  281.5 0.7 pad_maximum_fusion
  282.4 0.5 all-gather.13.cloned.1.call-update
  282.9 30.0 %all-gather.15.cloned.1.call-done = f32[3,6,32,512]{3,2,1,0:T(8,128)} async-done(((f32[3,6,32,128]{3,2,1,0:T(8,128)}), f32[3,6,32,512]{3,2,1,0:T(8,128)}) %all-gather.15.cloned.1.call-update) | async-done | bytes 1179664 | tf_op jit(solution)/shard_map/all_gather | solution.py:32
  312.9 5.1 convolution_bitcast_fusion.1
  318.0 0.7 all-gather.17.cloned.1.call-update
  318.8 0.2 all-reduce.3.cloned.1.call-start
  319.0 59.0 %all-gather.13.cloned.1.call-done = f32[6,6,512,128]{3,2,1,0:T(8,128)} async-done(((f32[6,6,32,128]{3,2,1,0:T(8,128)}), f32[6,6,512,128]{3,2,1,0:T(8,128)}) %all-gather.13.cloned.1.call-update) | async-done | bytes 9437200 | tf_op jit(solution)/shard_map/all_gather | solution.py:33
  378.0 10.1 %fusion.10 = f32[3,5,32,2,128]{4,2,3,1,0:T(8,128)S(1)} fusion(f32[3,2,6,512,128]{4,3,2,1,0:T(8,128)} %bitcast.107, f32[3,5,5,32,512]{4,3,2,1,0:T(8,128)} %all-gather.9.cloned.1.call-done), kind=kOutput, calls=%fused_computation.15 | convolution fusion | flops 3774873600 | bytes 13271040 | tf_op jit(solution)/shard_map/mstik,mctkj->mcsij/dot_general | solution.py:41
  388.0 2.6 fusion.16
  390.7 43.4 %reduce-scatter.5.cloned.1.call-done = f32[32,3,2,128]{3,0,2,1:T(8,128)} async-done(((f32[512,3,2,128]{3,0,2,1:T(8,128)}), f32[32,3,2,128]{3,0,2,1:T(8,128)}) %reduce-scatter.5.cloned.1.call-update) | async-done | bytes 98320 | tf_op jit(solution)/shard_map/reduce_scatter | solution.py:51
  434.1 2.4 fusion.28
  436.5 39.2 %all-gather.17.cloned.1.call-done = f32[6,6,32,512]{3,2,1,0:T(8,128)} async-done(((f32[6,6,32,128]{3,2,1,0:T(8,128)}), f32[6,6,32,512]{3,2,1,0:T(8,128)}) %all-gather.17.cloned.1.call-update) | async-done | bytes 2359312 | tf_op jit(solution)/shard_map/all_gather | solution.py:17
  475.7 3.4 convolution_bitcast_fusion
  479.1 2.1 copy.29
  481.3 0.6 dynamic-slice
  482.5 0.9 maximum_negate_fusion
  483.4 112.9 %all-reduce.3.cloned.1.call-done = f32[512,3,2,128]{3,2,1,0:T(2,128)} async-done(((f32[512,3,2,128]{3,2,1,0:T(2,128)}), f32[512,3,2,128]{3,2,1,0:T(2,128)}) %all-reduce.3.cloned.1.call-update) | async-done | bytes 1572880
  596.3 0.9 constant_dynamic-slice_fusion
  597.3 0.7 bitcast_subtract_fusion
  (34 shorter events, 0.5 us)
Async XLA Ops:
  7.2 1.6 copy-start.7
  7.2 101.0 %all-gather.7.cloned.1.call-start = ((), (), s32[]{:S(2)}) async-start(), calls=%async_computation.2 | async-start | bytes 11796480 | tf_op jit(solution)/shard_map/all_gather | solution.py:19
  7.9 106.3 %copy-start.3 = (f32[3,5,32,128]{3,2,1,0:T(8,128)S(1)}, f32[3,5,32,128]{3,2,1,0:T(8,128)}, u32[]{:S(2)}) copy-start(f32[3,5,32,128]{3,2,1,0:T(8,128)} %param.8) | copy-start | bytes 737284
  7.9 145.6 %all-gather.11.cloned.1.call-start = ((), (), s32[]{:S(2)}) async-start(), calls=%async_computation.4 | async-start | bytes 4177920 | tf_op jit(solution)/shard_map/all_gather | solution.py:14
  8.7 204.4 %all-gather.9.cloned.1.call-start = ((), (), s32[]{:S(2)}) async-start(), calls=%async_computation.3 | async-start | bytes 6144000 | tf_op jit(solution)/shard_map/all_gather | solution.py:21
  114.1 166.6 %reduce-scatter.3.cloned.1.call-start = ((), (), s32[]{:S(2)}) async-start(), calls=%async_computation.5 | async-start | bytes 835584 | tf_op jit(solution)/shard_map/reduce_scatter | solution.py:24
  221.1 96.9 %copy-start.2 = (f32[3,5,32,128]{3,2,1,0:T(8,128)}, f32[3,5,32,128]{3,2,1,0:T(8,128)S(1)}, u32[]{:S(2)}) copy-start(f32[3,5,32,128]{3,2,1,0:T(8,128)S(1)} %fusion.22) | copy-start | bytes 737284
  221.1 59.6 %copy-start.6 = (f32[3,32,128]{2,1,0:T(8,128)S(1)}, f32[3,32,128]{2,1,0:T(8,128)}, u32[]{:S(2)}) copy-start(f32[3,32,128]{2,1,0:T(8,128)} %param.9) | copy-start | bytes 147460
  221.1 91.8 %copy-start = (f32[6,6,32,128]{3,2,1,0:T(8,128)S(1)}, f32[6,6,32,128]{3,2,1,0:T(8,128)}, u32[]{:S(2)}) copy-start(f32[6,6,32,128]{3,2,1,0:T(8,128)} %param.10) | copy-start | bytes 1769476
  224.7 88.2 %all-gather.15.cloned.1.call-start = ((), (), s32[]{:S(2)}) async-start(), calls=%async_computation.7 | async-start | bytes 1474560 | tf_op jit(solution)/shard_map/all_gather | solution.py:32
  281.5 36.4 %copy-start.4 = (f32[3,32,128]{2,1,0:T(8,128)}, f32[3,32,128]{2,1,0:T(8,128)S(1)}, u32[]{:S(2)}) copy-start(f32[3,32,128]{2,1,0:T(8,128)S(1)} %bitcast_subtract_fusion.1) | copy-start | bytes 147460
  282.3 95.6 %all-gather.13.cloned.1.call-start = ((), (), s32[]{:S(2)}) async-start(), calls=%async_computation.6 | async-start | bytes 10027008 | tf_op jit(solution)/shard_map/all_gather | solution.py:33
  282.9 151.2 %reduce-scatter.5.cloned.1.call-start = ((), (), s32[]{:S(2)}) async-start(), calls=%async_computation.8 | async-start | bytes 1671168 | tf_op jit(solution)/shard_map/reduce_scatter | solution.py:51
  318.0 157.7 %all-gather.17.cloned.1.call-start = ((), (), s32[]{:S(2)}) async-start(), calls=%async_computation.9 | async-start | bytes 2949120 | tf_op jit(solution)/shard_map/all_gather | solution.py:17
  318.8 277.6 %all-reduce.3.cloned.1.call-start = ((), (), s32[]{:S(2)}) async-start(), calls=%async_computation.10 | async-start | bytes 3145728
  377.9 10.1 %copy-start.1 = (f32[3,6,32,512]{3,2,1,0:T(8,128)S(1)}, f32[3,6,32,512]{3,2,1,0:T(8,128)}, u32[]{:S(2)}) copy-start(f32[3,6,32,512]{3,2,1,0:T(8,128)} %all-gather.15.cloned.1.call-done) | copy-start | bytes 3538948
  479.0 2.2 copy-start.8
  481.2 116.0 %copy-start.5 = (f32[6,32,128]{2,1,0:T(8,128)S(1)}, f32[6,32,128]{2,1,0:T(8,128)}, u32[]{:S(2)}) copy-start(f32[6,32,128]{2,1,0:T(8,128)} %param.11) | copy-start | bytes 294916
Sparse Core Ops, SparseCore 0:
  9.8 98.3 all-gather.6
  110.0 43.3 all-gather.10
  155.3 57.7 all-gather.8
  224.9 55.8 reduce-scatter.2
  283.1 29.7 all-gather.14
  314.8 63.1 all-gather.12
  380.6 53.3 reduce-scatter.4
  435.9 39.7 all-gather.16
  481.4 114.9 all-reduce.2
where the time goes:
time: 605 us; the launch traced here: 604 us
  waiting for transfers between devices  528 us (87%)
  matrix products  35.1 us (6%)
  between operations  14.7 us (2%)
  blocking collectives  13.2 us (2%)
  local copies, waits for them, and re-layouts  9.73 us (2%)
    unnamed x10, waiting for transfers between devices  116 us
    all_gather x1, waiting for transfers between devices, on_device(): ancestors = lax.all_gather(anc_inverse, 'leaf', axis=0, tiled=True)  99.3 us
    all_gather x1, waiting for transfers between devices, on_device(): stripes = lax.all_gather(selected, 'col', axis=4, tiled=True)  59.6 us
    all_gather x1, waiting for transfers between devices, on_device(): two_rows = lax.all_gather(lower_two, 'row', axis=2, tiled=True)  59 us
    reduce_scatter x1, waiting for transfers between devices, on_device(): lax.psum_scatter(jnp.einsum('mski,mskj->imj', cols_piece, offdiag_one, pr...  55.9 us
    reduce_scatter x1, waiting for transfers between devices, on_device(): lax.psum_scatter(jnp.einsum('mqki,mcqkj->imcj', stripe_piece, local_split...  43.4 us
    all_gather x1, waiting for transfers between devices, on_device(): lax.all_gather(lower_two, 'col', axis=3, tiled=True)  39.2 us
    all_gather x1, waiting for transfers between devices, on_device(): parent_stripe = lax.all_gather(parent_col, 'col', axis=3, tiled=True)  30 us
  transfers between devices with their start and end apart: 9, of which 9 were waited for; matrix products, arithmetic and copies ran while one was open for 5% of the time, Pallas kernels for 0%

commit v1 on v0

--- a/solution.py
+++ b/solution.py
@@ -30,7 +30,12 @@
     diag_one = pivot_inv_one - jnp.transpose(summed_one, (1, 0, 2))
     parent_col = jnp.concatenate([offdiag_one, diag_one[:, None]], axis=1)
     parent_stripe = lax.all_gather(parent_col, "col", axis=3, tiled=True)
-    two_rows = lax.all_gather(lower_two, "row", axis=2, tiled=True)
+    ring = [lower_two]
+    for hop in range(15):
+        ring.append(lax.ppermute(ring[-1], "row", [(dev, (dev + 1) % 16) for dev in range(16)]))
+    two_rows = jnp.roll(
+        jnp.concatenate(ring[::-1], axis=2), (lax.axis_index("row") + 1) * ring[0].shape[2], axis=2
+    )
     rows_split = two_rows.reshape(
         level_nodes, children, struct_len + 1, two_rows.shape[2], tile_cols
     )

time: 605 us -> 578 us (0.955)
  waiting for transfers between devices: 528 us -> 408 us
  local copies, waits for them, and re-layouts: 9.73 us -> 70.5 us
  starting transfers between devices: 0.54 us -> 35.9 us
    ppermute x0 -> x15, waiting for transfers between devices: none -> 94.2 us  [on_device(): lax.ppermute(ring[-1], 'row', [(dev, (dev + 1) % 16) for dev in range(16)])]
    all_gather x1 -> x0, waiting for transfers between devices: 59 us -> none  [on_device(): two_rows = lax.all_gather(lower_two, 'row', axis=2, tiled=True)]
    unnamed x20 -> x71, local copies, waits for them, and re-layouts: 1.55 us -> 57.2 us
    reduce_scatter x1, waiting for transfers between devices: 43.4 us -> 0.02 us  [on_device(): lax.psum_scatter(jnp.einsum('mqki,mcqkj->imcj', stripe_piece, local_split...]
    all_gather x1, waiting for transfers between devices: 39.2 us -> 0.02 us  [on_device(): lax.all_gather(lower_two, 'col', axis=3, tiled=True)]
    ppermute x0 -> x15, starting transfers between devices: none -> 35.4 us  [on_device(): lax.ppermute(ring[-1], 'row', [(dev, (dev + 1) % 16) for dev in range(16)])]
    all_gather x1, waiting for transfers between devices: 26.1 us -> 0.01 us  [on_device(): one_rows = lax.all_gather(lower_one, 'row', axis=2, tiled=True)]
    reduce_scatter x1, waiting for transfers between devices: 55.9 us -> 33.9 us  [on_device(): lax.psum_scatter(jnp.einsum('mski,mskj->imj', cols_piece, offdiag_one, pr...]
  transfers between devices with their start and end apart: 9 -> 23, of which waited for: 9 -> 16; matrix products, arithmetic and copies ran while one was open for 5% -> 16% of each run, Pallas kernels for 0% -> 0%
where the time goes in v1:
time: 578 us; the launch traced here: 577 us
  waiting for transfers between devices  408 us (71%)
  local copies, waits for them, and re-layouts  70.5 us (12%)
  starting transfers between devices  35.9 us (6%)
  matrix products  29.7 us (5%)
  between operations  15.1 us (3%)
  blocking collectives  12.9 us (2%)
    unnamed x9, waiting for transfers between devices  119 us
    all_gather x1, waiting for transfers between devices, on_device(): ancestors = lax.all_gather(anc_inverse, 'leaf', axis=0, tiled=True)  98.6 us
    ppermute x15, waiting for transfers between devices, on_device(): lax.ppermute(ring[-1], 'row', [(dev, (dev + 1) % 16) for dev in range(16)])  94.2 us
    unnamed x71, local copies, waits for them, and re-layouts  57.2 us
    all_gather x1, waiting for transfers between devices, on_device(): stripes = lax.all_gather(selected, 'col', axis=4, tiled=True)  53.1 us
    ppermute x15, starting transfers between devices, on_device(): lax.ppermute(ring[-1], 'row', [(dev, (dev + 1) % 16) for dev in range(16)])  35.4 us
    reduce_scatter x1, waiting for transfers between devices, on_device(): lax.psum_scatter(jnp.einsum('mski,mskj->imj', cols_piece, offdiag_one, pr...  33.9 us
    all_gather x1, blocking collectives, on_device(): lax.all_gather(lower_one, 'col', axis=3, tiled=True)  12.9 us
  transfers between devices with their start and end apart: 23, of which 16 were waited for; matrix products, arithmetic and copies ran while one was open for 16% of the time, Pallas kernels for 0%

profile of v1, /device:TPU:1, one launch (start us, length us, event | category | flops | bytes accessed | tf_op | source)
XLA Modules:
  0.0 576.7 jit_solution(10665192730065724493)
XLA Ops:
  9.6 98.6 %all-gather.6.cloned.1.call-done = f32[24,24,32,128]{3,2,1,0:T(8,128)} async-done(((f32[6,24,32,128]{3,2,1,0:T(8,128)}), f32[24,24,32,128]{3,2,1,0:T(8,128)}) %all-gather.6.cloned.1.call-update) | async-done | bytes 9437200 | tf_op jit(solution)/shard_map/all_gather | solution.py:19
  108.2 5.9 %gather_fusion = f32[75,32,128]{2,1,0:T(8,128)} fusion(f32[24,24,32,128]{3,2,1,0:T(8,128)} %all-gather.6.cloned.1.call-done, s32[75]{0:T(128)S(1)} %reshape.41), kind=kCustom, calls=%fused_computation | custom fusion | bytes 2458200 | tf_op jit(solution)/shard_map/gather | solution.py:20
  116.0 8.4 %collective-permute-done = f32[6,6,32,128]{3,2,1,0:T(8,128)S(1)} collective-permute-done((f32[6,6,32,128]{3,2,1,0:T(8,128)}, f32[6,6,32,128]{3,2,1,0:T(8,128)S(1)}, u32[]{:S(2)}, u32[]{:S(2)}) %collective-permute-start) | collective-permute-done | bytes 589856 | tf_op jit(solution)/shard_map/ppermute | solution.py:35
  126.8 17.7 %collective-permute-done.1 = f32[6,6,32,128]{3,2,1,0:T(8,128)S(1)} collective-permute-done((f32[6,6,32,128]{3,2,1,0:T(8,128)S(1)}, f32[6,6,32,128]{3,2,1,0:T(8,128)S(1)}, u32[]{:S(2)}, u32[]{:S(2)}) %collective-permute-start.1) | collective-permute-done | bytes 589856 | tf_op jit(solution)/shard_map/ppermute | solution.py:35
  147.0 12.9 %all_gather.21 = f32[3,5,32,512]{3,2,1,0:T(8,128)S(1)} all-gather(f32[3,5,32,128]{3,2,1,0:T(8,128)} %param.8), channel_id=1, replica_groups=mesh['leaf'=4,'row'=16,'col'=4] {'col'}, dimensions={3}, use_global_device_ids=true | all-gather | bytes 1228800 | tf_op jit(solution)/shard_map/all_gather | solution.py:16
  161.6 53.1 %all-gather.8.cloned.1.call-done = f32[3,5,5,32,512]{4,3,2,1,0:T(8,128)} async-done(((f32[3,5,5,32,128]{4,3,2,1,0:T(8,128)}), f32[3,5,5,32,512]{4,3,2,1,0:T(8,128)}) %all-gather.8.cloned.1.call-update) | async-done | bytes 4915216 | tf_op jit(solution)/shard_map/all_gather | solution.py:21
  214.7 8.0 %fusion.19 = f32[3,5,32,128]{3,2,1,0:T(8,128)S(1)} fusion(f32[3,5,5,32,512]{4,3,2,1,0:T(8,128)} %all-gather.8.cloned.1.call-done, f32[3,5,512,128]{3,2,1,0:T(8,128)} %all-gather.10.cloned.1.call-done), kind=kOutput, calls=%fused_computation.18 | convolution fusion | flops 1887498240 | bytes 9093120 | tf_op jit(solution)/shard_map/mstik,mtkj->msij/dot_general | solution.py:22
  223.4 3.6 convolution_bitcast_fusion.2
  227.1 2.7 collective-permute-start.4
  229.8 7.1 %collective-permute-done.4 = f32[6,6,32,128]{3,2,1,0:T(8,128)S(1)} collective-permute-done((f32[6,6,32,128]{3,2,1,0:T(8,128)}, f32[6,6,32,128]{3,2,1,0:T(8,128)S(1)}, u32[]{:S(2)}, u32[]{:S(2)}) %collective-permute-start.4) | collective-permute-done | bytes 589856 | tf_op jit(solution)/shard_map/ppermute | solution.py:35
  239.3 7.6 %collective-permute-done.5 = f32[6,6,32,128]{3,2,1,0:T(8,128)} collective-permute-done((f32[6,6,32,128]{3,2,1,0:T(8,128)S(1)}, f32[6,6,32,128]{3,2,1,0:T(8,128)}, u32[]{:S(2)}, u32[]{:S(2)}) %collective-permute-start.5) | collective-permute-done | bytes 589856 | tf_op jit(solution)/shard_map/ppermute | solution.py:35
  246.9 2.7 collective-permute-start.6
  249.5 33.9 %reduce-scatter.3.cloned.1.call-done = f32[32,3,128]{2,0,1:T(8,128)} async-done(((f32[512,3,128]{2,0,1:T(8,128)}), f32[32,3,128]{2,0,1:T(8,128)}) %reduce-scatter.3.cloned.1.call-update) | async-done | bytes 49168 | tf_op jit(solution)/shard_map/reduce_scatter | solution.py:24
  287.5 7.1 %collective-permute-done.7 = f32[6,6,32,128]{3,2,1,0:T(8,128)S(1)} collective-permute-done((f32[6,6,32,128]{3,2,1,0:T(8,128)}, f32[6,6,32,128]{3,2,1,0:T(8,128)S(1)}, u32[]{:S(2)}, u32[]{:S(2)}) %collective-permute-start.7) | collective-permute-done | bytes 589856 | tf_op jit(solution)/shard_map/ppermute | solution.py:35
  297.9 6.8 %collective-permute-done.8 = f32[6,6,32,128]{3,2,1,0:T(8,128)} collective-permute-done((f32[6,6,32,128]{3,2,1,0:T(8,128)S(1)}, f32[6,6,32,128]{3,2,1,0:T(8,128)}, u32[]{:S(2)}, u32[]{:S(2)}) %collective-permute-start.8) | collective-permute-done | bytes 589856 | tf_op jit(solution)/shard_map/ppermute | solution.py:35
  304.7 2.6 collective-permute-start.9
  307.3 8.5 %all-gather.12.cloned.1.call-done = f32[3,6,32,512]{3,2,1,0:T(8,128)} async-done(((f32[3,6,32,128]{3,2,1,0:T(8,128)}), f32[3,6,32,512]{3,2,1,0:T(8,128)}) %all-gather.12.cloned.1.call-update) | async-done | bytes 1179664 | tf_op jit(solution)/shard_map/all_gather | solution.py:32
  315.8 5.0 convolution_bitcast_fusion.1
  320.9 2.7 collective-permute-start.10
  323.6 7.1 %collective-permute-done.10 = f32[6,6,32,128]{3,2,1,0:T(8,128)S(1)} collective-permute-done((f32[6,6,32,128]{3,2,1,0:T(8,128)}, f32[6,6,32,128]{3,2,1,0:T(8,128)S(1)}, u32[]{:S(2)}, u32[]{:S(2)}) %collective-permute-start.10) | collective-permute-done | bytes 589856 | tf_op jit(solution)/shard_map/ppermute | solution.py:35
  333.1 8.4 %collective-permute-done.11 = f32[6,6,32,128]{3,2,1,0:T(8,128)S(1)} collective-permute-done((f32[6,6,32,128]{3,2,1,0:T(8,128)S(1)}, f32[6,6,32,128]{3,2,1,0:T(8,128)S(1)}, u32[]{:S(2)}, u32[]{:S(2)}) %collective-permute-start.11) | collective-permute-done | bytes 589856 | tf_op jit(solution)/shard_map/ppermute | solution.py:35
  342.4 2.5 collective-permute-start.12
  344.9 8.1 %collective-permute-done.12 = f32[6,6,32,128]{3,2,1,0:T(8,128)S(1)} collective-permute-done((f32[6,6,32,128]{3,2,1,0:T(8,128)S(1)}, f32[6,6,32,128]{3,2,1,0:T(8,128)S(1)}, u32[]{:S(2)}, u32[]{:S(2)}) %collective-permute-start.12) | collective-permute-done | bytes 589856 | tf_op jit(solution)/shard_map/ppermute | solution.py:35
  353.8 2.6 collective-permute-start.13
  356.4 7.9 %collective-permute-done.13 = f32[6,6,32,128]{3,2,1,0:T(8,128)} collective-permute-done((f32[6,6,32,128]{3,2,1,0:T(8,128)S(1)}, f32[6,6,32,128]{3,2,1,0:T(8,128)}, u32[]{:S(2)}, u32[]{:S(2)}) %collective-permute-start.13) | collective-permute-done | bytes 589856 | tf_op jit(solution)/shard_map/ppermute | solution.py:35
  364.3 2.7 collective-permute-start.14
  367.3 7.9 %collective-permute-done.14 = f32[6,6,32,128]{3,2,1,0:T(8,128)} collective-permute-done((f32[6,6,32,128]{3,2,1,0:T(8,128)}, f32[6,6,32,128]{3,2,1,0:T(8,128)}, u32[]{:S(2)}, u32[]{:S(2)}) %collective-permute-start.14) | collective-permute-done | bytes 589856 | tf_op jit(solution)/shard_map/ppermute | solution.py:35
  406.5 2.6 constant_dynamic-update-slice_fusion.11
  426.2 4.4 constant_dynamic-slice_fusion.1
  434.3 5.9 %fusion.13 = f32[3,2,128,5,32]{2,4,3,1,0:T(8,128)S(1)} fusion(f32[3,2,128,5,32]{2,4,3,1,0:T(8,128)S(1)} %fusion.4, f32[3,5,5,32,512]{4,3,2,1,0:T(8,128)S(1)} %bitcast.110, f32[3,2,6,512,128]{4,3,2,1,0:T(8,128)S(1)} %bitcast.107), kind=kOutput, calls=%fused_computation.16 | convolution fusion | flops 3774996480 | bytes 13762560 | tf_op jit(solution)/shard_map/mstik,mctkj->mcsij/dot_general | solution.py:46
  442.7 3.4 convolution_bitcast_fusion
  450.4 117.9 %all-reduce.3.cloned.1.call-done = f32[512,3,2,128]{3,2,1,0:T(2,128)} async-done(((f32[512,3,2,128]{3,2,1,0:T(2,128)}), f32[512,3,2,128]{3,2,1,0:T(2,128)}) %all-reduce.3.cloned.1.call-update) | async-done | bytes 1572880
  (114 shorter events, 85.1 us)
Async XLA Ops:
  7.2 308.6 %copy-start.1 = (f32[6,6,32,128]{3,2,1,0:T(8,128)S(1)}, f32[6,6,32,128]{3,2,1,0:T(8,128)}, u32[]{:S(2)}) copy-start(f32[6,6,32,128]{3,2,1,0:T(8,128)} %param.10) | copy-start | bytes 1769476
  7.2 276.3 %copy-start.15 = (f32[3,32,128]{2,1,0:T(8,128)S(1)}, f32[3,32,128]{2,1,0:T(8,128)}, u32[]{:S(2)}) copy-start(f32[3,32,128]{2,1,0:T(8,128)} %param.9) | copy-start | bytes 147460
  7.2 101.0 %all-gather.6.cloned.1.call-start = ((), (), s32[]{:S(2)}) async-start(), calls=%async_computation.2 | async-start | bytes 11796480 | tf_op jit(solution)/shard_map/all_gather | solution.py:19
  7.9 153.6 %all-gather.10.cloned.1.call-start = ((), (), s32[]{:S(2)}) async-start(), calls=%async_computation.4 | async-start | bytes 4177920 | tf_op jit(solution)/shard_map/all_gather | solution.py:14
  8.7 206.0 %all-gather.8.cloned.1.call-start = ((), (), s32[]{:S(2)}) async-start(), calls=%async_computation.3 | async-start | bytes 6144000 | tf_op jit(solution)/shard_map/all_gather | solution.py:21
  114.1 285.9 %copy-start.2 = (f32[6,6,32,128]{3,2,1,0:T(8,128)S(1)}, f32[6,6,32,128]{3,2,1,0:T(8,128)}, u32[]{:S(2)}) copy-start(f32[6,6,32,128]{3,2,1,0:T(8,128)} %param.10) | copy-start | bytes 1769476
  114.1 169.3 %reduce-scatter.3.cloned.1.call-start = ((), (), s32[]{:S(2)}) async-start(), calls=%async_computation.5 | async-start | bytes 835584 | tf_op jit(solution)/shard_map/reduce_scatter | solution.py:24
  114.2 10.2 %collective-permute-start = (f32[6,6,32,128]{3,2,1,0:T(8,128)}, f32[6,6,32,128]{3,2,1,0:T(8,128)S(1)}, u32[]{:S(2)}, u32[]{:S(2)}) collective-permute-start(f32[6,6,32,128]{3,2,1,0:T(8,128)} %param.10), channel_id=1, source_target_pairs={{0,4},{4,8},{8,12},{12,16},{16,20},{20,24},{24,28},{28,32},{32,36}... | collective-permute-start | bytes 1769480 | tf_op jit(solution)/shard_map/ppermute | solution.py:35
  124.4 20.1 %collective-permute-start.1 = (f32[6,6,32,128]{3,2,1,0:T(8,128)S(1)}, f32[6,6,32,128]{3,2,1,0:T(8,128)S(1)}, u32[]{:S(2)}, u32[]{:S(2)}) collective-permute-start(f32[6,6,32,128]{3,2,1,0:T(8,128)S(1)} %collective-permute-done), channel_id=1, source_target_pairs={{0,4},{4,8},{8,12},{12,16},{16,20},{20,24},{24,28},{28,32},{32,36}... | collective-permute-start | bytes 1769480 | tf_op jit(solution)/shard_map/ppermute | solution.py:35
  144.5 15.4 %collective-permute-start.2 = (f32[6,6,32,128]{3,2,1,0:T(8,128)S(1)}, f32[6,6,32,128]{3,2,1,0:T(8,128)}, u32[]{:S(2)}, u32[]{:S(2)}) collective-permute-start(f32[6,6,32,128]{3,2,1,0:T(8,128)S(1)} %collective-permute-done.1), channel_id=1, source_target_pairs={{0,4},{4,8},{8,12},{12,16},{16,20},{20,24},{24,28},{28,32},{32,36}... | collective-permute-start | bytes 1769480 | tf_op jit(solution)/shard_map/ppermute | solution.py:35
  159.9 67.1 %collective-permute-start.3 = (f32[6,6,32,128]{3,2,1,0:T(8,128)}, f32[6,6,32,128]{3,2,1,0:T(8,128)}, u32[]{:S(2)}, u32[]{:S(2)}) collective-permute-start(f32[6,6,32,128]{3,2,1,0:T(8,128)} %collective-permute-done.2), channel_id=1, source_target_pairs={{0,4},{4,8},{8,12},{12,16},{16,20},{20,24},{24,28},{28,32},{32,36}... | collective-permute-start | bytes 1769480 | tf_op jit(solution)/shard_map/ppermute | solution.py:35
  227.0 88.7 %all-gather.12.cloned.1.call-start = ((), (), s32[]{:S(2)}) async-start(), calls=%async_computation.6 | async-start | bytes 1474560 | tf_op jit(solution)/shard_map/all_gather | solution.py:32
  227.1 9.9 %collective-permute-start.4 = (f32[6,6,32,128]{3,2,1,0:T(8,128)}, f32[6,6,32,128]{3,2,1,0:T(8,128)S(1)}, u32[]{:S(2)}, u32[]{:S(2)}) collective-permute-start(f32[6,6,32,128]{3,2,1,0:T(8,128)} %collective-permute-done.3), channel_id=1, source_target_pairs={{0,4},{4,8},{8,12},{12,16},{16,20},{20,24},{24,28},{28,32},{32,36}... | collective-permute-start | bytes 1769480 | tf_op jit(solution)/shard_map/ppermute | solution.py:35
  236.9 163.1 %copy-start.4 = (f32[6,6,32,128]{3,2,1,0:T(8,128)}, f32[6,6,32,128]{3,2,1,0:T(8,128)S(1)}, u32[]{:S(2)}) copy-start(f32[6,6,32,128]{3,2,1,0:T(8,128)S(1)} %collective-permute-done.4) | copy-start | bytes 1769476
  236.9 9.9 %collective-permute-start.5 = (f32[6,6,32,128]{3,2,1,0:T(8,128)S(1)}, f32[6,6,32,128]{3,2,1,0:T(8,128)}, u32[]{:S(2)}, u32[]{:S(2)}) collective-permute-start(f32[6,6,32,128]{3,2,1,0:T(8,128)S(1)} %collective-permute-done.4), channel_id=1, source_target_pairs={{0,4},{4,8},{8,12},{12,16},{16,20},{20,24},{24,28},{28,32},{32,36}... | collective-permute-start | bytes 1769480 | tf_op jit(solution)/shard_map/ppermute | solution.py:35
  246.9 39.2 %collective-permute-start.6 = (f32[6,6,32,128]{3,2,1,0:T(8,128)}, f32[6,6,32,128]{3,2,1,0:T(8,128)}, u32[]{:S(2)}, u32[]{:S(2)}) collective-permute-start(f32[6,6,32,128]{3,2,1,0:T(8,128)} %collective-permute-done.5), channel_id=1, source_target_pairs={{0,4},{4,8},{8,12},{12,16},{16,20},{20,24},{24,28},{28,32},{32,36}... | collective-permute-start | bytes 1769480 | tf_op jit(solution)/shard_map/ppermute | solution.py:35
  284.3 135.5 %copy-start.13 = (f32[3,32,128]{2,1,0:T(8,128)}, f32[3,32,128]{2,1,0:T(8,128)S(1)}, u32[]{:S(2)}) copy-start(f32[3,32,128]{2,1,0:T(8,128)S(1)} %bitcast_subtract_fusion.1) | copy-start | bytes 147460
  286.0 154.2 %reduce-scatter.5.cloned.1.call-start = ((), (), s32[]{:S(2)}) async-start(), calls=%async_computation.7 | async-start | bytes 1671168 | tf_op jit(solution)/shard_map/reduce_scatter | solution.py:56
  286.1 8.6 %collective-permute-start.7 = (f32[6,6,32,128]{3,2,1,0:T(8,128)}, f32[6,6,32,128]{3,2,1,0:T(8,128)S(1)}, u32[]{:S(2)}, u32[]{:S(2)}) collective-permute-start(f32[6,6,32,128]{3,2,1,0:T(8,128)} %collective-permute-done.6), channel_id=1, source_target_pairs={{0,4},{4,8},{8,12},{12,16},{16,20},{20,24},{24,28},{28,32},{32,36}... | collective-permute-start | bytes 1769480 | tf_op jit(solution)/shard_map/ppermute | solution.py:35
  295.5 9.2 %collective-permute-start.8 = (f32[6,6,32,128]{3,2,1,0:T(8,128)S(1)}, f32[6,6,32,128]{3,2,1,0:T(8,128)}, u32[]{:S(2)}, u32[]{:S(2)}) collective-permute-start(f32[6,6,32,128]{3,2,1,0:T(8,128)S(1)} %collective-permute-done.7), channel_id=1, source_target_pairs={{0,4},{4,8},{8,12},{12,16},{16,20},{20,24},{24,28},{28,32},{32,36}... | collective-permute-start | bytes 1769480 | tf_op jit(solution)/shard_map/ppermute | solution.py:35
  304.7 16.2 %collective-permute-start.9 = (f32[6,6,32,128]{3,2,1,0:T(8,128)}, f32[6,6,32,128]{3,2,1,0:T(8,128)}, u32[]{:S(2)}, u32[]{:S(2)}) collective-permute-start(f32[6,6,32,128]{3,2,1,0:T(8,128)} %collective-permute-done.8), channel_id=1, source_target_pairs={{0,4},{4,8},{8,12},{12,16},{16,20},{20,24},{24,28},{28,32},{32,36}... | collective-permute-start | bytes 1769480 | tf_op jit(solution)/shard_map/ppermute | solution.py:35
  320.8 121.9 %all-gather.14.cloned.1.call-start = ((), (), s32[]{:S(2)}) async-start(), calls=%async_computation.8 | async-start | bytes 2949120 | tf_op jit(solution)/shard_map/all_gather | solution.py:17
  320.9 9.9 %collective-permute-start.10 = (f32[6,6,32,128]{3,2,1,0:T(8,128)}, f32[6,6,32,128]{3,2,1,0:T(8,128)S(1)}, u32[]{:S(2)}, u32[]{:S(2)}) collective-permute-start(f32[6,6,32,128]{3,2,1,0:T(8,128)} %collective-permute-done.9), channel_id=1, source_target_pairs={{0,4},{4,8},{8,12},{12,16},{16,20},{20,24},{24,28},{28,32},{32,36}... | collective-permute-start | bytes 1769480 | tf_op jit(solution)/shard_map/ppermute | solution.py:35
  330.7 69.2 %copy-start.7 = (f32[6,6,32,128]{3,2,1,0:T(8,128)}, f32[6,6,32,128]{3,2,1,0:T(8,128)S(1)}, u32[]{:S(2)}) copy-start(f32[6,6,32,128]{3,2,1,0:T(8,128)S(1)} %collective-permute-done.10) | copy-start | bytes 1769476
  330.8 10.8 %collective-permute-start.11 = (f32[6,6,32,128]{3,2,1,0:T(8,128)S(1)}, f32[6,6,32,128]{3,2,1,0:T(8,128)S(1)}, u32[]{:S(2)}, u32[]{:S(2)}) collective-permute-start(f32[6,6,32,128]{3,2,1,0:T(8,128)S(1)} %collective-permute-done.10), channel_id=1, source_target_pairs={{0,4},{4,8},{8,12},{12,16},{16,20},{20,24},{24,28},{28,32},{32,36}... | collective-permute-start | bytes 1769480 | tf_op jit(solution)/shard_map/ppermute | solution.py:35
  342.4 10.6 %collective-permute-start.12 = (f32[6,6,32,128]{3,2,1,0:T(8,128)S(1)}, f32[6,6,32,128]{3,2,1,0:T(8,128)S(1)}, u32[]{:S(2)}, u32[]{:S(2)}) collective-permute-start(f32[6,6,32,128]{3,2,1,0:T(8,128)S(1)} %collective-permute-done.11), channel_id=1, source_target_pairs={{0,4},{4,8},{8,12},{12,16},{16,20},{20,24},{24,28},{28,32},{32,36}... | collective-permute-start | bytes 1769480 | tf_op jit(solution)/shard_map/ppermute | solution.py:35
  353.8 10.5 %collective-permute-start.13 = (f32[6,6,32,128]{3,2,1,0:T(8,128)S(1)}, f32[6,6,32,128]{3,2,1,0:T(8,128)}, u32[]{:S(2)}, u32[]{:S(2)}) collective-permute-start(f32[6,6,32,128]{3,2,1,0:T(8,128)S(1)} %collective-permute-done.12), channel_id=1, source_target_pairs={{0,4},{4,8},{8,12},{12,16},{16,20},{20,24},{24,28},{28,32},{32,36}... | collective-permute-start | bytes 1769480 | tf_op jit(solution)/shard_map/ppermute | solution.py:35
  364.3 10.9 %collective-permute-start.14 = (f32[6,6,32,128]{3,2,1,0:T(8,128)}, f32[6,6,32,128]{3,2,1,0:T(8,128)}, u32[]{:S(2)}, u32[]{:S(2)}) collective-permute-start(f32[6,6,32,128]{3,2,1,0:T(8,128)} %collective-permute-done.13), channel_id=1, source_target_pairs={{0,4},{4,8},{8,12},{12,16},{16,20},{20,24},{24,28},{28,32},{32,36}... | collective-permute-start | bytes 1769480 | tf_op jit(solution)/shard_map/ppermute | solution.py:35
  367.1 201.2 %all-reduce.3.cloned.1.call-start = ((), (), s32[]{:S(2)}) async-start(), calls=%async_computation.9 | async-start | bytes 3145728
  367.3 38.3 %copy-start.9 = (f32[6,6,32,128]{3,2,1,0:T(8,128)S(1)}, f32[6,6,32,128]{3,2,1,0:T(8,128)}, u32[]{:S(2)}) copy-start(f32[6,6,32,128]{3,2,1,0:T(8,128)} %copy-done.8) | copy-start | bytes 1769476
  367.3 45.7 %copy-start.6 = (f32[6,6,32,128]{3,2,1,0:T(8,128)S(1)}, f32[6,6,32,128]{3,2,1,0:T(8,128)}, u32[]{:S(2)}) copy-start(f32[6,6,32,128]{3,2,1,0:T(8,128)} %copy-done.5) | copy-start | bytes 1769476
  430.6 138.6 %copy-start.14 = (f32[6,32,128]{2,1,0:T(8,128)S(1)}, f32[6,32,128]{2,1,0:T(8,128)}, u32[]{:S(2)}) copy-start(f32[6,32,128]{2,1,0:T(8,128)} %param.11) | copy-start | bytes 294916
  (10 other events, 132.8 us)
Sparse Core Ops, SparseCore 0:
  9.8 98.3 all-gather.5
  110.1 45.7 all-gather.9
  157.6 57.0 all-gather.7
  227.1 56.2 reduce-scatter.2
  286.1 29.5 all-gather.11
  321.0 58.4 reduce-scatter.4
  381.3 39.2 all-gather.13
  448.4 119.8 all-reduce.2
